TPU v7x, 256 devices: a whole 4x4x8 slice. The times are simulated.
256 devices in a mesh: wide: 32 (over y, z), grp: 8 (over x, core).
Axes of the slice: x: 4, y: 4, z: 8, core: 2. Of those that a mesh axis runs over, the one named last changes fastest.
Arguments:
- tokens: bfloat16 [65536, 8192], P('wide', 'grp'), may hold values from -6 to 6
- value_weight: bfloat16 [8192, 1024], P('grp'), may hold values from -0.09375 to 0.09375
- down_panel_table: bfloat16 [1280, 64, 8192], P('wide', None, 'grp'), may hold values from -0.0625 to 0.0625
- up_panel_table: bfloat16 [1280, 64, 1024], P('wide', None, 'grp'), may hold values from -0.75 to 0.75
- request_adapter: int32 [32, 32], P('wide'), may hold values from 0 to 1279, as said below
- request_length: int32 [32, 32], P('wide'), may hold values from 1 to 128, 2048 in all within a row
- adapter_panel_place: int32 [1280], replicated, may hold values from 0 to 1279, as said below
Outputs:
- values_out: bfloat16 [65536, 1024], P('wide', 'grp')
Inputs may be any that keep to these rules, and one draw needn't show every extreme that they name: `request_adapter`: each index of wide has at most 2 requests whose adapters share one owner; in every draw some owner receives exactly 2 from every index of wide. `request_length`: each row sums to 2048, and holds a request of exactly 128 rows. `adapter_panel_place`: A permutation of the adapters' panel slots.
All inputs are finite; a program needn't handle non-finite values.
Results may differ from a plain program's by a relative error of at most 0.0044.
Values may be sent and summed in bfloat16 or wider, within the bound.
A program may use at most 192 MiB of HBM per device.

v0:
```python
import jax
import jax.numpy as jnp
from jax import lax
from jax.sharding import PartitionSpec as P

ADP_W = 40
BLOCK = 128


def down_then_up(token_blocks, down_panels, up_panels):
    value_partial = jnp.einsum(
        "cuq,cgq->cug", token_blocks, down_panels, preferred_element_type=jnp.float32
    )
    slot_count, block_rows, rank_width = value_partial.shape
    summed = lax.psum(value_partial.reshape(slot_count, block_rows * rank_width), "grp")
    rank_projected = summed.reshape(slot_count, block_rows, rank_width).astype(jnp.bfloat16)
    return jnp.einsum(
        "lvk,lkn->lvn", rank_projected, up_panels, preferred_element_type=jnp.float32
    ).astype(jnp.bfloat16)


def shards(
    tokens,
    value_weight,
    down_panel_table,
    up_panel_table,
    request_adapter,
    request_length,
    adapter_panel_place,
):
    owners = lax.axis_size("wide")
    token_count, feature_width = tokens.shape
    block_rows = BLOCK
    requests = request_adapter.shape[1]
    capacity = 2 * requests // owners
    slot_total = owners * capacity
    output_width = up_panel_table.shape[2]
    adapters = request_adapter[0]
    lengths = request_length[0]
    table_size = adapter_panel_place.shape[0]
    lookup = adapters[:, None] == jnp.arange(table_size)[None, :]
    panel_slot = jnp.sum(jnp.where(lookup, adapter_panel_place[None, :], 0), axis=1)
    owner_index = panel_slot // ADP_W
    local_index = panel_slot % ADP_W
    starts = jnp.cumsum(lengths) - lengths
    onehot = (owner_index[:, None] == jnp.arange(owners)[None, :]).astype(jnp.int32)
    earlier = jnp.cumsum(onehot, axis=0) - onehot
    owner_rank = jnp.sum(earlier * onehot, axis=1)
    slot_place = owner_index * capacity + owner_rank
    matches = slot_place[None, :] == jnp.arange(slot_total)[:, None]
    slot_start = jnp.sum(jnp.where(matches, starts[None, :], 0), axis=1)
    slot_length = jnp.sum(jnp.where(matches, lengths[None, :], 0), axis=1)
    slot_local = jnp.sum(jnp.where(matches, local_index[None, :], 0), axis=1)
    offsets = jnp.arange(block_rows)
    inside_rows = offsets[None, :] < slot_length[:, None]
    source_rows = jnp.where(inside_rows, slot_start[:, None] + offsets[None, :], 0).reshape(-1)
    send_rows = jnp.where(
        inside_rows.reshape(-1, 1), tokens[source_rows], jnp.zeros((), tokens.dtype)
    )
    positions = jnp.arange(token_count)
    ends = starts + lengths
    inside = (positions[:, None] >= starts[None, :]) & (positions[:, None] < ends[None, :])
    token_dest = jnp.sum(
        jnp.where(
            inside, slot_place[None, :] * block_rows - starts[None, :] + positions[:, None], 0
        ),
        axis=1,
    )
    ids_received = lax.all_to_all(
        slot_local.reshape(owners, capacity), "wide", split_axis=0, concat_axis=0, tiled=True
    )
    base_term = jnp.dot(tokens, value_weight, preferred_element_type=jnp.float32)
    base_sum = lax.psum_scatter(base_term, "grp", scatter_dimension=1, tiled=True)
    arrived = lax.all_to_all(
        send_rows.reshape(owners, capacity * block_rows, feature_width),
        "wide",
        split_axis=0,
        concat_axis=0,
        tiled=True,
    )
    flattened_adapter_ids = ids_received.reshape(-1)
    token_blocks = arrived.reshape(slot_total, block_rows, feature_width)
    block_deltas = down_then_up(
        token_blocks, down_panel_table[flattened_adapter_ids], up_panel_table[flattened_adapter_ids]
    )
    returned = lax.all_to_all(
        block_deltas.reshape(owners, capacity * block_rows, output_width),
        "wide",
        split_axis=0,
        concat_axis=0,
        tiled=True,
    )
    delta_flat = returned.reshape(slot_total * block_rows, output_width)
    token_delta = delta_flat[token_dest]
    return (base_sum + token_delta.astype(jnp.float32)).astype(jnp.bfloat16)


def solution(mesh):
    placed = (
        P("wide", "grp"),
        P("grp", None),
        P("wide", None, "grp"),
        P("wide", None, "grp"),
        P("wide", None),
        P("wide", None),
        P(),
    )
    return jax.shard_map(
        shards, mesh=mesh, in_specs=placed, out_specs=P("wide", "grp"), check_vma=False
    )
```

profile of v0, /device:TPU:33, one launch (start us, length us, event | category | flops | bytes accessed | tf_op | source)
XLA Modules:
  0.0 642.9 jit_solution(14910857943977885815)
XLA Ops:
  6.5 1.0 select_reduce_fusion.1
  7.6 0.1 fusion.1
  7.7 0.2 select_reduce_fusion.5
  7.9 0.7 copy.16
  8.7 0.1 reduce
  8.8 0.7 subtract_bitcast_fusion
  9.5 0.8 select_reduce_fusion.2
  10.3 0.7 all_to_all.13
  11.0 10.8 %all-to-all-start.1 = ((s32[32,1,2]{2,1,0:T(1,128)}), s32[32,1,2]{2,1,0:T(1,128)S(1)}, u32[]{:S(2)}, u32[]{:S(2)}) async-start(s32[32,1,2]{2,1,0:T(1,128)} %bitcast.8), calls=%async_computation.2 | async-start | bytes 32768 | tf_op jit(solution)/shard_map/all_to_all | solution.py:69
  21.8 0.1 lt.95
  21.9 0.1 add_select_fusion
  22.1 43.4 %gather_fusion = bf16[8192,1024]{1,0:T(8,128)(2,1)} fusion(bf16[2048,1024]{1,0:T(8,128)(2,1)} %param.7, s32[8192]{0:T(1024)S(1)} %broadcast_clamp_fusion), kind=kCustom, calls=%fused_computation | custom fusion | bytes 33587200 | tf_op jit(solution)/shard_map/gather | solution.py:58
  65.5 0.1 lt.96
  65.6 14.1 %broadcast_select_fusion = bf16[32,256,1024]{2,1,0:T(8,128)(2,1)} fusion(bf16[32,256,1024]{2,1,0:T(8,128)(2,1)} %bitcast.49, pred[32,256]{1,0:T(8,128)(4,1)S(1)} %bitcast_compare_fusion), kind=kLoop, calls=%fused_computation.4 | loop fusion | flops 8388608 | bytes 33562624 | tf_op jit(solution)/shard_map/jit(_where)/select_n | solution.py:57
  79.7 9.3 %all-to-all-start = ((bf16[32,256,1024]{2,1,0:T(8,128)(2,1)}), bf16[32,256,1024]{2,1,0:T(8,128)(2,1)}, u32[]{:S(2)}, u32[]{:S(2)}) async-start(bf16[32,256,1024]{2,1,0:T(8,128)(2,1)} %broadcast_select_fusion), calls=%async_computation.1 | async-start | bytes 33554432 | tf_op jit(solution)/shard_map/all_to_all | solution.py:74
  89.0 9.0 %fusion.6 = f32[2048,1024]{1,0:T(8,128)} fusion(bf16[2048,1024]{1,0:T(8,128)(2,1)} %param.7, bf16[1024,1024]{1,0:T(8,128)(2,1)S(1)} %copy-done), kind=kOutput, calls=%fused_computation.41 | convolution fusion | flops 4294967296 | bytes 14680064 | tf_op jit(solution)/shard_map/dot_general | solution.py:72
  98.0 0.5 broadcast.213
  98.6 0.7 reduce.5
  99.3 0.1 reshape.226
  99.4 8.0 %gather_fusion.1 = bf16[64,64,1024]{2,1,0:T(8,128)(2,1)} fusion(bf16[40,64,1024]{2,1,0:T(8,128)(2,1)} %param.9, s32[1024]{0:T(1024)S(1)} %pad_clamp_fusion), kind=kCustom, calls=%fused_computation.1 | custom fusion | bytes 16777472 | tf_op jit(solution)/shard_map/gather | solution.py:84
  107.4 1.7 gather_fusion.2
  109.0 358.1 %all-to-all-done = bf16[32,256,1024]{2,1,0:T(8,128)(2,1)} async-done(((bf16[32,256,1024]{2,1,0:T(8,128)(2,1)}), bf16[32,256,1024]{2,1,0:T(8,128)(2,1)}, u32[]{:S(2)}, u32[]{:S(2)}) %all-to-all-start) | async-done | bytes 16777248 | tf_op jit(solution)/shard_map/all_to_all | solution.py:74
  467.2 11.8 %fusion.7 = f32[64,128,64]{2,1,0:T(8,128)} fusion(bf16[64,128,1024]{2,1,0:T(8,128)(2,1)} %bitcast.7, bf16[64,64,1024]{2,1,0:T(8,128)(2,1)} %gather_fusion.1), kind=kOutput, calls=%fused_computation.42 | convolution fusion | flops 1073741824 | bytes 27262976 | tf_op jit(solution)/shard_map/cuq,cgq->cug/dot_general | solution.py:11
  479.0 4.8 reshape.227
  483.8 53.0 %all-reduce.1 = bf16[64,8192]{1,0:T(8,128)(2,1)S(1)} all-reduce(f32[64,8192]{1,0:T(8,128)} %reshape.227), channel_id=1, replica_groups=mesh['wide'=32,'grp'=8] {'grp'}, use_global_device_ids=true, to_apply=%region_8.9 | all-reduce | flops 524288 | bytes 3145728 | tf_op jit(solution)/shard_map/psum | solution.py:15
  536.8 3.3 convert_element_type.20
  540.0 3.9 convolution_convert_fusion
  543.9 36.4 %all-to-all-start.2 = ((bf16[32,256,128]{2,1,0:T(8,128)(2,1)}), bf16[32,256,128]{2,1,0:T(8,128)(2,1)}, u32[]{:S(2)}, u32[]{:S(2)}) async-start(bf16[32,256,128]{2,1,0:T(8,128)(2,1)} %bitcast.50), calls=%async_computation.3 | async-start | bytes 4194304 | tf_op jit(solution)/shard_map/all_to_all | solution.py:86
  580.4 0.2 select_reduce_fusion
  580.6 45.8 %all-to-all-done.2 = bf16[32,256,128]{2,1,0:T(8,128)(2,1)} async-done(((bf16[32,256,128]{2,1,0:T(8,128)(2,1)}), bf16[32,256,128]{2,1,0:T(8,128)(2,1)}, u32[]{:S(2)}, u32[]{:S(2)}) %all-to-all-start.2) | async-done | bytes 2097184 | tf_op jit(solution)/shard_map/all_to_all | solution.py:86
  626.4 7.5 %gather_fusion.3 = bf16[2048,128]{1,0:T(8,128)(2,1)S(1)} fusion(bf16[8192,128]{1,0:T(8,128)(2,1)} %bitcast.11, s32[2048]{0:T(1024)S(1)} %broadcast_clamp_fusion.1), kind=kCustom, calls=%fused_computation.3 | custom fusion | bytes 1056768 | tf_op jit(solution)/shard_map/gather | solution.py:94
  633.9 2.1 add_convert_fusion
  (21 shorter events, 0.3 us)
Async XLA Ops:
  6.5 82.5 %copy-start = (bf16[1024,1024]{1,0:T(8,128)(2,1)S(1)}, bf16[1024,1024]{1,0:T(8,128)(2,1)}, u32[]{:S(2)}) copy-start(bf16[1024,1024]{1,0:T(8,128)(2,1)} %param.8) | copy-start | bytes 6291460
  11.0 68.7 %all-to-all-start.1 = ((s32[32,1,2]{2,1,0:T(1,128)}), s32[32,1,2]{2,1,0:T(1,128)S(1)}, u32[]{:S(2)}, u32[]{:S(2)}) async-start(s32[32,1,2]{2,1,0:T(1,128)} %bitcast.8), calls=%async_computation.2 | async-start | bytes 32768 | tf_op jit(solution)/shard_map/all_to_all | solution.py:69
  79.7 387.5 %all-to-all-start = ((bf16[32,256,1024]{2,1,0:T(8,128)(2,1)}), bf16[32,256,1024]{2,1,0:T(8,128)(2,1)}, u32[]{:S(2)}, u32[]{:S(2)}) async-start(bf16[32,256,1024]{2,1,0:T(8,128)(2,1)} %broadcast_select_fusion), calls=%async_computation.1 | async-start | bytes 33554432 | tf_op jit(solution)/shard_map/all_to_all | solution.py:74
  89.0 544.9 %reduce-scatter.2.cloned.1.call-start = ((), (), s32[]{:S(2)}) async-start(), calls=%async_computation.4 | async-start | bytes 9437184 | tf_op jit(solution)/shard_map/reduce_scatter | solution.py:73
  99.4 8.0 %copy-start.1 = (bf16[40,64,128]{2,1,0:T(8,128)(2,1)S(1)}, bf16[40,64,128]{2,1,0:T(8,128)(2,1)}, u32[]{:S(2)}) copy-start(bf16[40,64,128]{2,1,0:T(8,128)(2,1)} %param.10) | copy-start | bytes 1966084
  543.9 82.5 %all-to-all-start.2 = ((bf16[32,256,128]{2,1,0:T(8,128)(2,1)}), bf16[32,256,128]{2,1,0:T(8,128)(2,1)}, u32[]{:S(2)}, u32[]{:S(2)}) async-start(bf16[32,256,128]{2,1,0:T(8,128)(2,1)} %bitcast.50), calls=%async_computation.3 | async-start | bytes 4194304 | tf_op jit(solution)/shard_map/all_to_all | solution.py:86
Sparse Core Ops, SparseCore 0:
  98.2 56.5 reduce-scatter.1
where the time goes:
time: 649 us; the launch traced here: 643 us
  waiting for transfers between devices  404 us (62%)
  local copies, waits for them, and re-layouts  70.8 us (11%)
  starting transfers between devices  56.6 us (9%)
  blocking collectives  53 us (8%)
  matrix products  24.7 us (4%)
  other arithmetic  20.2 us (3%)
  between operations  13.6 us (2%)
    all_to_all x1, waiting for transfers between devices, shards(): lax.all_to_all(send_rows.reshape(owners, capacity * block_rows, feature_w...  358 us
    psum x1, blocking collectives, down_then_up(): lax.psum(value_partial.reshape(slot_count, block_rows * rank_width), 'grp')  53 us
    all_to_all x1, waiting for transfers between devices, shards(): lax.all_to_all(block_deltas.reshape(owners, capacity * block_rows, output...  45.8 us
    gather x1, local copies, waits for them, and re-layouts, shards(): tokens[source_rows]  43.4 us
    all_to_all x1, starting transfers between devices, shards(): lax.all_to_all(block_deltas.reshape(owners, capacity * block_rows, output...  36.4 us
    select_n x1, other arithmetic, shards(): jnp.where(inside_rows.reshape(-1, 1), tokens[source_rows], jnp.zeros((),...  14.1 us
  transfers between devices with their start and end apart: 4, of which 2 were waited for; matrix products, arithmetic and copies ran while one was open for 17% of the time, Pallas kernels for 0%

commit v1 on v0

v1 whole, which is shorter than its diff:
```python
import functools

import jax
import jax.numpy as jnp
from jax import lax
from jax.experimental import pallas as pl
from jax.experimental.pallas import tpu as pltpu
from jax.sharding import PartitionSpec as P

MESH = pl.DeviceIdType.MESH
ADP_W = 40
F32 = jnp.float32
BF16 = jnp.bfloat16
ROWS = 512


def routes(request_adapter, request_length, adapter_panel_place):
    adapters, lengths = request_adapter[0], request_length[0]
    count = adapters.shape[0]
    lookup = adapters[:, None] == jnp.arange(adapter_panel_place.shape[0])[None, :]
    panel_slot = jnp.sum(jnp.where(lookup, adapter_panel_place[None, :], 0), axis=1)
    owner = panel_slot // ADP_W
    local = panel_slot - owner * ADP_W
    before = jnp.arange(count)[None, :] < jnp.arange(count)[:, None]
    starts = jnp.sum(jnp.where(before, lengths[None, :], 0), axis=1)
    same = owner[None, :] == owner[:, None]
    rank = jnp.sum(jnp.where(before & same, 1, 0), axis=1)
    place = owner * 2 + rank
    matches = place[None, :] == jnp.arange(128)[:, None]
    ids = jnp.sum(jnp.where(matches, local[None, :], 0), axis=1)
    return ids.astype(jnp.int32)[None, :], jnp.stack([starts, place]).astype(jnp.int32)


def kernel(
    owners,
    groups,
    ids_ref,
    meta_ref,
    tokens_hbm,
    weight_hbm,
    down_hbm,
    up_hbm,
    out_ref,
    tokens,
    weight,
    down,
    up,
    stage,
    stage_up,
    held,
    held_up,
    base_send,
    base_held,
    acc,
    code,
    packed,
    packed_held,
    rounded,
    ids_all,
    ids_smem,
    load_sem,
    ids_send,
    ids_recv,
    down_send,
    down_recv,
    up_send,
    up_recv,
    base_ssem,
    base_rsem,
    part_ssem,
    part_rsem,
    full_ssem,
    full_rsem,
):
    me = lax.axis_index("wide")
    grp = lax.axis_index("grp")
    my_y, my_z = me // 8, me % 8
    my_x, core = grp // 2, grp % 2
    tokens_n = tokens.shape[0]
    steps = owners - 1

    def offset(i):
        zi, dy = i // 4, (i % 4 + 1) % 4
        dz = (4 - (zi + 1) // 2) * (2 * (zi % 2) - 1) * (1 - 2 * core)
        return dy, dz

    def target(i):
        dy, dz = offset(i)
        return ((my_y + dy) % 4) * 8 + (my_z + dz + 8) % 8

    def source(i):
        dy, dz = offset(i)
        return ((my_y - dy + 4) % 4) * 8 + (my_z - dz + 8) % 8

    loads = [
        pltpu.make_async_copy(down_hbm, down, load_sem.at[0]),
        pltpu.make_async_copy(up_hbm, up, load_sem.at[1]),
        pltpu.make_async_copy(tokens_hbm, tokens, load_sem.at[2]),
        pltpu.make_async_copy(weight_hbm, weight, load_sem.at[3]),
    ]
    for load in loads:
        load.start()
    own_ids = pltpu.make_async_copy(ids_ref, ids_all.at[me], load_sem.at[4])
    own_ids.start()

    barrier = pltpu.get_barrier_semaphore()

    @pl.loop(0, steps)
    def _(i):
        pl.semaphore_signal(barrier, 1, device_id=(target(i), grp), device_id_type=MESH)

    @pl.loop(1, groups)
    def _(k):
        pl.semaphore_signal(barrier, 1, device_id=(me, (grp + k) % groups), device_id_type=MESH)

    pl.semaphore_wait(barrier, steps + groups - 1)

    def ids_copy(i):
        return pltpu.make_async_remote_copy(
            ids_ref, ids_all.at[me], ids_send.at[i], ids_recv.at[i],
            device_id=(target(i), grp), device_id_type=MESH,
        )

    @pl.loop(0, steps)
    def _(i):
        ids_copy(i).start()

    own_ids.wait()

    def ids_arrival(i):
        return pltpu.make_async_remote_copy(
            ids_ref, ids_all.at[source(i)], ids_send.at[i], ids_recv.at[i],
            device_id=(target(i), grp), device_id_type=MESH,
        )

    @pl.loop(0, steps)
    def _(i):
        ids_arrival(i).wait()

    to_smem = pltpu.make_async_copy(ids_all, ids_smem, load_sem.at[5])
    to_smem.start()
    to_smem.wait()
    loads[0].wait()

    def down_copy(i):
        return pltpu.make_async_remote_copy(
            stage.at[i], held.at[i], down_send.at[i], down_recv.at[i],
            device_id=(target(i), grp), device_id_type=MESH,
        )

    def up_copy(i):
        return pltpu.make_async_remote_copy(
            stage_up.at[i], held_up.at[i], up_send.at[i], up_recv.at[i],
            device_id=(target(i), grp), device_id_type=MESH,
        )

    @pl.loop(0, steps)
    def _(i):
        to = target(i)
        stage[i, 0:64] = down[ids_smem[to, 0, 2 * me]]
        stage[i, 64:128] = down[ids_smem[to, 0, 2 * me + 1]]
        down_copy(i).start()

    held[steps, 0:64] = down[ids_smem[me, 0, 2 * me]]
    held[steps, 64:128] = down[ids_smem[me, 0, 2 * me + 1]]
    loads[1].wait()

    @pl.loop(0, steps)
    def _(i):
        to = target(i)
        stage_up[i, 0:64] = up[ids_smem[to, 0, 2 * me]]
        stage_up[i, 64:128] = up[ids_smem[to, 0, 2 * me + 1]]
        up_copy(i).start()

    held_up[steps, 0:64] = up[ids_smem[me, 0, 2 * me]]
    held_up[steps, 64:128] = up[ids_smem[me, 0, 2 * me + 1]]

    def base_copy(k, c):
        slot = 2 * k + c
        return pltpu.make_async_remote_copy(
            base_send.at[slot], base_held.at[2 * k + core], base_ssem.at[slot], base_rsem.at[2 * k + core],
            device_id=(me, ((my_x + k) % 4) * 2 + c), device_id_type=MESH,
        )

    def base_arrival(k, c):
        slot = 2 * k + c
        return pltpu.make_async_remote_copy(
            base_send.at[slot], base_held.at[slot], base_ssem.at[slot], base_rsem.at[slot],
            device_id=(me, ((my_x + k) % 4) * 2 + c), device_id_type=MESH,
        )

    loads[2].wait()
    loads[3].wait()

    @pl.loop(0, 4)
    def _(k):
        columns = pl.ds(pl.multiple_of(((my_x + k) % 4) * 256, 256), 256)

        @pl.loop(0, tokens_n // ROWS)
        def _(m):
            rows = pl.ds(pl.multiple_of(m * ROWS, ROWS), ROWS)
            part = jnp.dot(tokens[rows, :], weight[:, columns], preferred_element_type=F32)
            base_send[2 * k, rows] = part[:, :128]
            base_send[2 * k + 1, rows] = part[:, 128:]

        @pl.when(k == 0)
        def _():
            base_copy(0, 1 - core).start()

        @pl.when(k > 0)
        def _():
            base_copy(k, 0).start()
            base_copy(k, 1).start()

    lane = lax.broadcasted_iota(jnp.int32, (ROWS, 128), 1)
    row = lax.broadcasted_iota(jnp.int32, (ROWS, 128), 0)
    upper = jnp.where(lane < 64, 0, 1)

    @pl.loop(0, tokens_n // ROWS)
    def _(m):
        rows = pl.ds(pl.multiple_of(m * ROWS, ROWS), ROWS)
        at = row + m * ROWS
        slot = lax.fori_loop(
            0, meta_ref.shape[1],
            lambda r, s: jnp.where(at >= meta_ref[0, r], meta_ref[1, r], s),
            jnp.zeros((ROWS, 128), jnp.int32),
        )
        code[rows] = slot - upper
        acc[rows] = jnp.zeros((ROWS, 128), F32)

    @pl.loop(0, owners // 2)
    def _(j):
        down_copy(2 * j).wait_recv()

        @pl.when(2 * j + 1 < steps)
        def _():
            down_copy(2 * j + 1).wait_recv()

        first, second = 2 * source(2 * j), 2 * source(2 * j + 1)

        @pl.loop(0, tokens_n // ROWS)
        def _(m):
            rows = pl.ds(pl.multiple_of(m * ROWS, ROWS), ROWS)
            panels = held[pl.ds(2 * j, 2)].reshape(256, held.shape[2])
            part = lax.dot_general(
                tokens[rows, :], panels, (((1,), (1,)), ((), ())), preferred_element_type=F32
            )
            at = code[rows]
            acc[rows] += jnp.where(at == first, part[:, :128], 0.0) + jnp.where(at == second, part[:, 128:], 0.0)

    half = lax.broadcasted_iota(jnp.int32, (128, 128), 1) < 64

    @pl.loop(0, groups)
    def _(p):
        top = acc[pl.ds(pl.multiple_of(p * 256, 256), 128)]
        low = acc[pl.ds(pl.multiple_of(p * 256 + 128, 128), 128)]
        packed[p] = jnp.where(half, top + pltpu.roll(top, 64, 1), low + pltpu.roll(low, 64, 1))

    def part_copy(k):
        to = (grp + k) % groups
        return pltpu.make_async_remote_copy(
            packed.at[to], packed_held.at[k], part_ssem.at[k], part_rsem.at[k],
            device_id=(me, to), device_id_type=MESH,
        )

    @pl.loop(1, groups)
    def _(k):
        part_copy(k).start()

    @pl.loop(0, 4)
    def _(k):
        @pl.when(k == 0)
        def _():
            base_arrival(0, 1 - core).wait_recv()

        @pl.when(k > 0)
        def _():
            base_arrival(k, 0).wait_recv()
            base_arrival(k, 1).wait_recv()

    @pl.loop(0, tokens_n // ROWS)
    def _(m):
        rows = pl.ds(pl.multiple_of(m * ROWS, ROWS), ROWS)
        total = base_send[core, rows] + base_held[1 - core, rows]
        for slot in range(2, 8):
            total = total + base_held[slot, rows]
        base_held[core, rows] = total
        acc[rows] = jnp.zeros((ROWS, 128), F32)

    total = packed[grp]

    def add_part(k, s):
        part_copy(k).wait_recv()
        return s + packed_held[k]

    rounded[grp] = lax.fori_loop(1, groups, add_part, total).astype(BF16)

    def full_copy(k):
        return pltpu.make_async_remote_copy(
            rounded.at[grp], rounded.at[grp], full_ssem.at[k], full_rsem.at[k],
            device_id=(me, (grp + k) % groups), device_id_type=MESH,
        )

    def full_arrival(k):
        source_of = (grp + groups - k) % groups
        return pltpu.make_async_remote_copy(
            rounded.at[source_of], rounded.at[source_of], full_ssem.at[k], full_rsem.at[k],
            device_id=(me, (grp + k) % groups), device_id_type=MESH,
        )

    @pl.loop(1, groups)
    def _(k):
        full_copy(k).start()

    @pl.loop(1, groups)
    def _(k):
        full_arrival(k).wait_recv()

    shrunk = base_send.at[1 - core]

    @pl.loop(1, groups)
    def _(k):
        part_copy(k).wait_send()

    base_copy(0, 1 - core).wait_send()

    @pl.loop(0, groups)
    def _(p):
        both = rounded[p].astype(F32)
        other = pltpu.roll(both, 64, 1)
        shrunk[pl.ds(pl.multiple_of(p * 256, 256), 128)] = jnp.where(half, both, other)
        shrunk[pl.ds(pl.multiple_of(p * 256 + 128, 128), 128)] = jnp.where(half, other, both)

    @pl.loop(0, owners // 4)
    def _(j):
        for a in range(3):
            up_copy(4 * j + a).wait_recv()

        @pl.when(4 * j + 3 < steps)
        def _():
            up_copy(4 * j + 3).wait_recv()

        names = [2 * source(4 * j + a) for a in range(4)]

        @pl.loop(0, tokens_n // ROWS)
        def _(m):
            rows = pl.ds(pl.multiple_of(m * ROWS, ROWS), ROWS)
            at, value = code[rows], shrunk[rows]
            spread = jnp.concatenate([jnp.where(at == n, value, 0.0).astype(BF16) for n in names], axis=1)
            panels = held_up[pl.ds(4 * j, 4)].reshape(512, 128)
            acc[rows] += jnp.dot(spread, panels, preferred_element_type=F32)

    @pl.loop(0, tokens_n // ROWS)
    def _(m):
        rows = pl.ds(pl.multiple_of(m * ROWS, ROWS), ROWS)
        out_ref[rows] = (base_held[core, rows] + acc[rows].astype(BF16).astype(F32)).astype(BF16)

    @pl.loop(0, steps)
    def _(i):
        down_copy(i).wait_send()
        up_copy(i).wait_send()

    @pl.loop(1, groups)
    def _(k):
        full_copy(k).wait_send()

    @pl.loop(1, 4)
    def _(k):
        base_copy(k, 0).wait_send()
        base_copy(k, 1).wait_send()


def shards(tokens, value_weight, down_panels, up_panels, request_adapter, request_length, adapter_panel_place):
    owners, groups = lax.axis_size("wide"), lax.axis_size("grp")
    ids, meta = routes(request_adapter, request_length, adapter_panel_place)
    rows, features = tokens.shape
    units = up_panels.shape[2]
    dma = pltpu.SemaphoreType.DMA
    vmem = pltpu.VMEM
    return pl.pallas_call(
        functools.partial(kernel, owners, groups),
        out_shape=jax.ShapeDtypeStruct((rows, units), BF16),
        in_specs=[
            pl.BlockSpec(memory_space=pltpu.VMEM),
            pl.BlockSpec(memory_space=pltpu.SMEM),
        ]
        + [pl.BlockSpec(memory_space=pl.ANY)] * 4,
        out_specs=pl.BlockSpec(memory_space=pltpu.VMEM),
        scratch_shapes=[
            vmem(tokens.shape, BF16),
            vmem(value_weight.shape, BF16),
            vmem(down_panels.shape, BF16),
            vmem(up_panels.shape, BF16),
            vmem((owners - 1, 128, features), BF16),
            vmem((owners - 1, 128, units), BF16),
            vmem((owners, 128, features), BF16),
            vmem((owners, 128, units), BF16),
            vmem((groups, rows, units), F32),
            vmem((groups, rows, units), F32),
            vmem((rows, 128), F32),
            vmem((rows, 128), jnp.int32),
            vmem((groups, 128, 128), F32),
            vmem((groups, 128, 128), F32),
            vmem((groups, 128, 128), BF16),
            vmem((owners, 1, 128), jnp.int32),
            pltpu.SMEM((owners, 1, 128), jnp.int32),
            dma((6,)),
            dma((owners - 1,)),
            dma((owners - 1,)),
            dma((owners - 1,)),
            dma((owners - 1,)),
            dma((owners - 1,)),
            dma((owners - 1,)),
            dma((groups,)),
            dma((groups,)),
            dma((groups,)),
            dma((groups,)),
            dma((groups,)),
            dma((groups,)),
        ],
        compiler_params=pltpu.CompilerParams(
            collective_id=0, has_side_effects=True, vmem_limit_bytes=60 * 2**20
        ),
        name="routed_lora",
    )(ids, meta, tokens, value_weight, down_panels, up_panels)


def solution(mesh):
    placed = (
        P("wide", "grp"),
        P("grp", None),
        P("wide", None, "grp"),
        P("wide", None, "grp"),
        P("wide", None),
        P("wide", None),
        P(),
    )
    return jax.shard_map(
        shards, mesh=mesh, in_specs=placed, out_specs=P("wide", "grp"), check_vma=False
    )
```

time: 649 us -> 264 us (0.41)
  waiting for transfers between devices: 404 us -> 0 us
  Pallas kernels: 0 us -> 259 us
  local copies, waits for them, and re-layouts: 70.8 us -> 1.87 us
  starting transfers between devices: 56.6 us -> 0 us
  blocking collectives: 53 us -> 0 us
  matrix products: 24.7 us -> 0 us
  other arithmetic: 20.2 us -> 3.13 us
  between operations: 13.6 us -> 0.03 us
    all_to_all x3 -> x0, waiting for transfers between devices: 404 us -> none  [the longest x1 358 us: shards(): lax.all_to_all(send_rows.reshape(owners, capacity * block_rows, feature_w...]
    pallas_call x0 -> x1, Pallas kernels: none -> 259 us  [shards(): pl.pallas_call(functools.partial(kernel, owners, groups), out_shape=jax.S...]
    gather x4 -> x0, local copies, waits for them, and re-layouts: 60.5 us -> none  [the longest x1 43.4 us: shards(): tokens[source_rows]]
    all_to_all x3 -> x0, starting transfers between devices: 56.5 us -> none  [the longest x1 36.4 us: shards(): lax.all_to_all(block_deltas.reshape(owners, capacity * block_rows, output...]
    psum x1 -> x0, blocking collectives: 53 us -> none  [down_then_up(): lax.psum(value_partial.reshape(slot_count, block_rows * rank_width), 'grp')]
    dot_general x3 -> x0, matrix products: 24.7 us -> none  [the longest x1 11.8 us: down_then_up(): jnp.einsum('cuq,cgq->cug', token_blocks, down_panels, preferred_element_t...]
    select_n x6 -> x0, other arithmetic: 14.2 us -> none  [the longest x1 14.1 us: shards(): jnp.where(inside_rows.reshape(-1, 1), tokens[source_rows], jnp.zeros((),...]
  transfers between devices with their start and end apart: 4 -> 0, of which waited for: 2 -> 0; matrix products, arithmetic and copies ran while one was open for 17% -> 0% of each run, Pallas kernels for 0% -> 0%
where the time goes in v1:
time: 264 us
  Pallas kernels  259 us (98%)
  other arithmetic  3.13 us (1%)
    pallas_call x1, Pallas kernels, shards(): pl.pallas_call(functools.partial(kernel, owners, groups), out_shape=jax.S...  259 us

profile of v1, /device:TPU:33, one launch (start us, length us, event | category | flops | bytes accessed | tf_op | source)
XLA Modules:
  0.0 264.3 jit_solution(17419141025129330576)
XLA Ops:
  0.0 0.9 select_reduce_fusion
  0.9 0.8 select_reduce_fusion.1
  1.7 0.2 select_reduce_fusion.3
  1.9 0.7 select_reduce_fusion.2
  2.6 0.6 pad_add_fusion.meta_ref
  3.2 259.2 %routed_lora.1 = bf16[2048,128]{1,0:T(8,128)(2,1)} custom-call(s32[1,128]{1,0:T(1,128)} %bitcast.14, s32[2,32]{1,0:T(2,128)} %pad_add_fusion.meta_ref, bf16[2048,1024]{1,0:T(8,128)(2,1)} %tokens_hbm.1, bf16[1024,1024]{1,0:T(8,128)(2,1)} %weight_hbm.1, bf16[40,64,1024]{2,1,0:T(8,128)(2,1)} %down_hbm.1, bf16[40,64,128]{2,1,0:T(8,128)(2,1)} %up_hbm.1), custom_call_target="tpu_custom_call" | custom-call | tf_op jit(solution)/shard_map/routed_lora/pallas_call | solution.py:380
  262.4 1.9 copy.9
  (3 shorter events, 0.0 us)

commit v2 on v1

--- a/solution.py
+++ b/solution.py
@@ -14,28 +14,12 @@
 ROWS = 512
 
 
-def routes(request_adapter, request_length, adapter_panel_place):
-    adapters, lengths = request_adapter[0], request_length[0]
-    count = adapters.shape[0]
-    lookup = adapters[:, None] == jnp.arange(adapter_panel_place.shape[0])[None, :]
-    panel_slot = jnp.sum(jnp.where(lookup, adapter_panel_place[None, :], 0), axis=1)
-    owner = panel_slot // ADP_W
-    local = panel_slot - owner * ADP_W
-    before = jnp.arange(count)[None, :] < jnp.arange(count)[:, None]
-    starts = jnp.sum(jnp.where(before, lengths[None, :], 0), axis=1)
-    same = owner[None, :] == owner[:, None]
-    rank = jnp.sum(jnp.where(before & same, 1, 0), axis=1)
-    place = owner * 2 + rank
-    matches = place[None, :] == jnp.arange(128)[:, None]
-    ids = jnp.sum(jnp.where(matches, local[None, :], 0), axis=1)
-    return ids.astype(jnp.int32)[None, :], jnp.stack([starts, place]).astype(jnp.int32)
-
-
 def kernel(
     owners,
     groups,
-    ids_ref,
-    meta_ref,
+    adapter_ref,
+    length_ref,
+    place_ref,
     tokens_hbm,
     weight_hbm,
     down_hbm,
@@ -56,8 +40,10 @@
     packed,
     packed_held,
     rounded,
+    ids_ref,
     ids_all,
     ids_smem,
+    meta_ref,
     load_sem,
     ids_send,
     ids_recv,
@@ -80,8 +66,9 @@
     steps = owners - 1
 
     def offset(i):
-        zi, dy = i // 4, (i % 4 + 1) % 4
-        dz = (4 - (zi + 1) // 2) * (2 * (zi % 2) - 1) * (1 - 2 * core)
+        n = i % 8
+        dy = (i // 8 + n + 2) % 4
+        dz = (4 - n + 3 * (n // 4)) * (1 - 2 * (n % 2)) * (1 - 2 * core)
         return dy, dz
 
     def target(i):
@@ -100,19 +87,35 @@
     ]
     for load in loads:
         load.start()
+
+    barrier = pltpu.get_barrier_semaphore()
+
+    @pl.loop(0, steps)
+    def _(i):
+        pl.semaphore_signal(barrier, 1, device_id=(target(i), grp), device_id_type=MESH)
+
+    @pl.loop(1, groups)
+    def _(k):
+        pl.semaphore_signal(barrier, 1, device_id=(me, (grp + k) % groups), device_id_type=MESH)
+
+    lanes = lax.broadcasted_iota(jnp.int32, (1, 128), 1)
+    lane_owner, lane_turn = lanes // 2, lanes % 2
+    count = adapter_ref.shape[1]
+
+    def route(r, state):
+        ids, turn, start = state
+        panel = place_ref[adapter_ref[0, r]]
+        owner = panel // ADP_W
+        meta_ref[0, r] = start
+        meta_ref[1, r] = owner
+        hit = lane_owner == owner
+        ids = jnp.where(hit & (lane_turn == turn), panel - owner * ADP_W, ids)
+        return ids, jnp.where(hit, turn + 1, turn), start + length_ref[0, r]
+
+    nothing = jnp.zeros((1, 128), jnp.int32)
+    ids_ref[...] = lax.fori_loop(0, count, route, (nothing, nothing, 0))[0]
     own_ids = pltpu.make_async_copy(ids_ref, ids_all.at[me], load_sem.at[4])
     own_ids.start()
-
-    barrier = pltpu.get_barrier_semaphore()
-
-    @pl.loop(0, steps)
-    def _(i):
-        pl.semaphore_signal(barrier, 1, device_id=(target(i), grp), device_id_type=MESH)
-
-    @pl.loop(1, groups)
-    def _(k):
-        pl.semaphore_signal(barrier, 1, device_id=(me, (grp + k) % groups), device_id_type=MESH)
-
     pl.semaphore_wait(barrier, steps + groups - 1)
 
     def ids_copy(i):
@@ -216,20 +219,26 @@
     row = lax.broadcasted_iota(jnp.int32, (ROWS, 128), 0)
     upper = jnp.where(lane < 64, 0, 1)
 
+    @pl.loop(0, count)
+    def _(r):
+        def earlier(q, rank):
+            return rank + jnp.where((meta_ref[1, q] == meta_ref[1, r]) & (q < r), 1, 0)
+
+        meta_ref[2, r] = 2 * meta_ref[1, r] + lax.fori_loop(0, count, earlier, 0)
+
     @pl.loop(0, tokens_n // ROWS)
     def _(m):
         rows = pl.ds(pl.multiple_of(m * ROWS, ROWS), ROWS)
         at = row + m * ROWS
         slot = lax.fori_loop(
-            0, meta_ref.shape[1],
-            lambda r, s: jnp.where(at >= meta_ref[0, r], meta_ref[1, r], s),
+            0, count,
+            lambda r, s: jnp.where(at >= meta_ref[0, r], meta_ref[2, r], s),
             jnp.zeros((ROWS, 128), jnp.int32),
         )
         code[rows] = slot - upper
         acc[rows] = jnp.zeros((ROWS, 128), F32)
 
-    @pl.loop(0, owners // 2)
-    def _(j):
+    def shrink(j):
         down_copy(2 * j).wait_recv()
 
         @pl.when(2 * j + 1 < steps)
@@ -238,9 +247,9 @@
 
         first, second = 2 * source(2 * j), 2 * source(2 * j + 1)
 
-        @pl.loop(0, tokens_n // ROWS)
+        @pl.loop(0, tokens_n // 1024)
         def _(m):
-            rows = pl.ds(pl.multiple_of(m * ROWS, ROWS), ROWS)
+            rows = pl.ds(pl.multiple_of(m * 1024, 1024), 1024)
             panels = held[pl.ds(2 * j, 2)].reshape(256, held.shape[2])
             part = lax.dot_general(
                 tokens[rows, :], panels, (((1,), (1,)), ((), ())), preferred_element_type=F32
@@ -248,107 +257,115 @@
             at = code[rows]
             acc[rows] += jnp.where(at == first, part[:, :128], 0.0) + jnp.where(at == second, part[:, 128:], 0.0)
 
-    half = lax.broadcasted_iota(jnp.int32, (128, 128), 1) < 64
-
-    @pl.loop(0, groups)
-    def _(p):
-        top = acc[pl.ds(pl.multiple_of(p * 256, 256), 128)]
-        low = acc[pl.ds(pl.multiple_of(p * 256 + 128, 128), 128)]
-        packed[p] = jnp.where(half, top + pltpu.roll(top, 64, 1), low + pltpu.roll(low, 64, 1))
-
-    def part_copy(k):
-        to = (grp + k) % groups
-        return pltpu.make_async_remote_copy(
-            packed.at[to], packed_held.at[k], part_ssem.at[k], part_rsem.at[k],
-            device_id=(me, to), device_id_type=MESH,
-        )
-
-    @pl.loop(1, groups)
-    def _(k):
-        part_copy(k).start()
-
-    @pl.loop(0, 4)
-    def _(k):
-        @pl.when(k == 0)
-        def _():
-            base_arrival(0, 1 - core).wait_recv()
-
-        @pl.when(k > 0)
-        def _():
-            base_arrival(k, 0).wait_recv()
-            base_arrival(k, 1).wait_recv()
-
-    @pl.loop(0, tokens_n // ROWS)
+    @pl.loop(0, owners // 2 - 4)
+    def _(j):
+        shrink(j)
+
+    base_arrival(0, 1 - core).wait_recv()
+
+    @pl.loop(1, 4)
+    def _(k):
+        base_arrival(k, 0).wait_recv()
+        base_arrival(k, 1).wait_recv()
+
+    @pl.loop(0, tokens_n // 256)
     def _(m):
-        rows = pl.ds(pl.multiple_of(m * ROWS, ROWS), ROWS)
+        rows = pl.ds(pl.multiple_of(m * 256, 256), 256)
         total = base_send[core, rows] + base_held[1 - core, rows]
         for slot in range(2, 8):
             total = total + base_held[slot, rows]
         base_held[core, rows] = total
+
+    @pl.loop(owners // 2 - 4, owners // 2)
+    def _(j):
+        shrink(j)
+
+    half = lax.broadcasted_iota(jnp.int32, (128, 128), 1) < 64
+
+    def pack(k):
+        p = (grp + k) % groups
+        top = acc[pl.ds(pl.multiple_of(p * 256, 256), 128)]
+        low = acc[pl.ds(pl.multiple_of(p * 256 + 128, 128), 128)]
+        packed[k] = jnp.where(half, top + pltpu.roll(top, 64, 1), low + pltpu.roll(low, 64, 1))
+
+    def part_copy(k):
+        return pltpu.make_async_remote_copy(
+            packed.at[k], packed_held.at[k], part_ssem.at[k], part_rsem.at[k],
+            device_id=(me, (grp + k) % groups), device_id_type=MESH,
+        )
+
+    @pl.loop(1, groups)
+    def _(k):
+        pack(k)
+        part_copy(k).start()
+
+    pack(0)
+
+    @pl.loop(0, tokens_n // ROWS)
+    def _(m):
+        rows = pl.ds(pl.multiple_of(m * ROWS, ROWS), ROWS)
         acc[rows] = jnp.zeros((ROWS, 128), F32)
 
-    total = packed[grp]
+    total = packed[0]
 
     def add_part(k, s):
         part_copy(k).wait_recv()
         return s + packed_held[k]
 
-    rounded[grp] = lax.fori_loop(1, groups, add_part, total).astype(BF16)
+    rounded[0] = lax.fori_loop(1, groups, add_part, total).astype(BF16)
 
     def full_copy(k):
         return pltpu.make_async_remote_copy(
-            rounded.at[grp], rounded.at[grp], full_ssem.at[k], full_rsem.at[k],
+            rounded.at[0], rounded.at[k], full_ssem.at[k], full_rsem.at[k],
             device_id=(me, (grp + k) % groups), device_id_type=MESH,
         )
 
-    def full_arrival(k):
-        source_of = (grp + groups - k) % groups
-        return pltpu.make_async_remote_copy(
-            rounded.at[source_of], rounded.at[source_of], full_ssem.at[k], full_rsem.at[k],
-            device_id=(me, (grp + k) % groups), device_id_type=MESH,
-        )
-
     @pl.loop(1, groups)
     def _(k):
         full_copy(k).start()
 
-    @pl.loop(1, groups)
-    def _(k):
-        full_arrival(k).wait_recv()
-
     shrunk = base_send.at[1 - core]
-
-    @pl.loop(1, groups)
-    def _(k):
-        part_copy(k).wait_send()
-
     base_copy(0, 1 - core).wait_send()
 
-    @pl.loop(0, groups)
-    def _(p):
-        both = rounded[p].astype(F32)
+    @pl.loop(1, 4)
+    def _(k):
+        base_copy(k, 0).wait_send()
+        base_copy(k, 1).wait_send()
+
+    def unpack(k):
+        p = (grp + groups - k) % groups
+        both = rounded[k].astype(F32)
         other = pltpu.roll(both, 64, 1)
         shrunk[pl.ds(pl.multiple_of(p * 256, 256), 128)] = jnp.where(half, both, other)
         shrunk[pl.ds(pl.multiple_of(p * 256 + 128, 128), 128)] = jnp.where(half, other, both)
 
-    @pl.loop(0, owners // 4)
-    def _(j):
-        for a in range(3):
-            up_copy(4 * j + a).wait_recv()
-
-        @pl.when(4 * j + 3 < steps)
-        def _():
-            up_copy(4 * j + 3).wait_recv()
-
-        names = [2 * source(4 * j + a) for a in range(4)]
+    unpack(0)
+
+    @pl.loop(1, groups)
+    def _(k):
+        full_copy(k).wait_recv()
+        unpack(k)
+
+    def apply(j):
+        @pl.loop(0, 8)
+        def _(a):
+            @pl.when(8 * j + a < steps)
+            def _():
+                up_copy(8 * j + a).wait_recv()
+
+        names = [2 * source(8 * j + a) for a in range(8)]
 
         @pl.loop(0, tokens_n // ROWS)
         def _(m):
             rows = pl.ds(pl.multiple_of(m * ROWS, ROWS), ROWS)
             at, value = code[rows], shrunk[rows]
             spread = jnp.concatenate([jnp.where(at == n, value, 0.0).astype(BF16) for n in names], axis=1)
-            panels = held_up[pl.ds(4 * j, 4)].reshape(512, 128)
+            panels = held_up[pl.ds(8 * j, 8)].reshape(8 * 128, 128)
             acc[rows] += jnp.dot(spread, panels, preferred_element_type=F32)
+
+    @pl.loop(0, owners // 8)
+    def _(j):
+        apply(j)
 
     @pl.loop(0, tokens_n // ROWS)
     def _(m):
@@ -362,17 +379,12 @@
 
     @pl.loop(1, groups)
     def _(k):
+        part_copy(k).wait_send()
         full_copy(k).wait_send()
-
-    @pl.loop(1, 4)
-    def _(k):
-        base_copy(k, 0).wait_send()
-        base_copy(k, 1).wait_send()
 
 
 def shards(tokens, value_weight, down_panels, up_panels, request_adapter, request_length, adapter_panel_place):
     owners, groups = lax.axis_size("wide"), lax.axis_size("grp")
-    ids, meta = routes(request_adapter, request_length, adapter_panel_place)
     rows, features = tokens.shape
     units = up_panels.shape[2]
     dma = pltpu.SemaphoreType.DMA
@@ -381,7 +393,8 @@
         functools.partial(kernel, owners, groups),
         out_shape=jax.ShapeDtypeStruct((rows, units), BF16),
         in_specs=[
-            pl.BlockSpec(memory_space=pltpu.VMEM),
+            pl.BlockSpec(memory_space=pltpu.SMEM),
+            pl.BlockSpec(memory_space=pltpu.SMEM),
             pl.BlockSpec(memory_space=pltpu.SMEM),
         ]
         + [pl.BlockSpec(memory_space=pl.ANY)] * 4,
@@ -402,8 +415,10 @@
             vmem((groups, 128, 128), F32),
             vmem((groups, 128, 128), F32),
             vmem((groups, 128, 128), BF16),
+            vmem((1, 128), jnp.int32),
             vmem((owners, 1, 128), jnp.int32),
             pltpu.SMEM((owners, 1, 128), jnp.int32),
+            pltpu.SMEM((3, request_adapter.shape[1]), jnp.int32),
             dma((6,)),
             dma((owners - 1,)),
             dma((owners - 1,)),
@@ -422,7 +437,7 @@
             collective_id=0, has_side_effects=True, vmem_limit_bytes=60 * 2**20
         ),
         name="routed_lora",
-    )(ids, meta, tokens, value_weight, down_panels, up_panels)
+    )(request_adapter, request_length, adapter_panel_place, tokens, value_weight, down_panels, up_panels)
 
 
 def solution(mesh):

time: 264 us -> 232 us (0.88)
  Pallas kernels: 259 us -> 229 us
  other arithmetic: 3.13 us -> 0 us
    pallas_call x1, Pallas kernels: 259 us -> 229 us  [shards(): pl.pallas_call(functools.partial(kernel, owners, groups), out_shape=jax.S...]
where the time goes in v2:
time: 232 us; the launch traced here: 231 us
  Pallas kernels  229 us (99%)
    pallas_call x1, Pallas kernels, shards(): pl.pallas_call(functools.partial(kernel, owners, groups), out_shape=jax.S...  229 us

profile of v2, /device:TPU:33, one launch (start us, length us, event | category | flops | bytes accessed | tf_op | source)
XLA Modules:
  0.0 231.4 jit_solution(5953450561853555351)
XLA Ops:
  0.0 229.5 %routed_lora.1 = bf16[2048,128]{1,0:T(8,128)(2,1)} custom-call(s32[1,32]{1,0:T(1,128)} %adapter_ref.1, s32[1,32]{1,0:T(1,128)} %length_ref.1, s32[1280]{0:T(1024)} %place_ref.1, bf16[2048,1024]{1,0:T(8,128)(2,1)} %tokens_hbm.1, bf16[1024,1024]{1,0:T(8,128)(2,1)} %weight_hbm.1, bf16[40,64,1024]{2,1,0:T(8,128)(2,1)} %down_hbm.1, bf16[40,64,128]{2,1,0:T(8,128)(2,1)} %up_hbm.1), custom_call_target="tpu_custom_call" | custom-call | tf_op jit(solution)/shard_map/routed_lora/pallas_call | solution.py:392
  229.5 1.9 copy.9

commit v3 on v2

--- a/solution.py
+++ b/solution.py
@@ -11,15 +11,15 @@
 ADP_W = 40
 F32 = jnp.float32
 BF16 = jnp.bfloat16
-ROWS = 512
+ROWS = 1024
 
 
 def kernel(
     owners,
     groups,
-    adapter_ref,
-    length_ref,
-    place_ref,
+    adapter_hbm,
+    length_hbm,
+    place_hbm,
     tokens_hbm,
     weight_hbm,
     down_hbm,
@@ -40,6 +40,9 @@
     packed,
     packed_held,
     rounded,
+    adapter_ref,
+    length_ref,
+    place_ref,
     ids_ref,
     ids_all,
     ids_smem,
@@ -79,6 +82,13 @@
         dy, dz = offset(i)
         return ((my_y - dy + 4) % 4) * 8 + (my_z - dz + 8) % 8
 
+    tables = [
+        pltpu.make_async_copy(adapter_hbm, adapter_ref, load_sem.at[6]),
+        pltpu.make_async_copy(length_hbm, length_ref, load_sem.at[7]),
+        pltpu.make_async_copy(place_hbm, place_ref, load_sem.at[8]),
+    ]
+    for table in tables:
+        table.start()
     loads = [
         pltpu.make_async_copy(down_hbm, down, load_sem.at[0]),
         pltpu.make_async_copy(up_hbm, up, load_sem.at[1]),
@@ -90,8 +100,7 @@
 
     barrier = pltpu.get_barrier_semaphore()
 
-    @pl.loop(0, steps)
-    def _(i):
+    for i in range(steps):
         pl.semaphore_signal(barrier, 1, device_id=(target(i), grp), device_id_type=MESH)
 
     @pl.loop(1, groups)
@@ -112,6 +121,8 @@
         ids = jnp.where(hit & (lane_turn == turn), panel - owner * ADP_W, ids)
         return ids, jnp.where(hit, turn + 1, turn), start + length_ref[0, r]
 
+    for table in tables:
+        table.wait()
     nothing = jnp.zeros((1, 128), jnp.int32)
     ids_ref[...] = lax.fori_loop(0, count, route, (nothing, nothing, 0))[0]
     own_ids = pltpu.make_async_copy(ids_ref, ids_all.at[me], load_sem.at[4])
@@ -124,8 +135,7 @@
             device_id=(target(i), grp), device_id_type=MESH,
         )
 
-    @pl.loop(0, steps)
-    def _(i):
+    for i in range(steps):
         ids_copy(i).start()
 
     own_ids.wait()
@@ -136,8 +146,7 @@
             device_id=(target(i), grp), device_id_type=MESH,
         )
 
-    @pl.loop(0, steps)
-    def _(i):
+    for i in range(steps):
         ids_arrival(i).wait()
 
     to_smem = pltpu.make_async_copy(ids_all, ids_smem, load_sem.at[5])
@@ -346,31 +355,36 @@
         full_copy(k).wait_recv()
         unpack(k)
 
-    def apply(j):
-        @pl.loop(0, 8)
+    def arrive(first, count_up):
+        @pl.loop(0, count_up)
         def _(a):
-            @pl.when(8 * j + a < steps)
+            @pl.when(first + a < steps)
             def _():
-                up_copy(8 * j + a).wait_recv()
-
-        names = [2 * source(8 * j + a) for a in range(8)]
+                up_copy(first + a).wait_recv()
+
+    def term(first, count_up, rows):
+        names = [2 * source(first + a) for a in range(count_up)]
+        at, value = code[rows], shrunk[rows]
+        spread = jnp.concatenate([jnp.where(at == n, value, 0.0).astype(BF16) for n in names], axis=1)
+        panels = held_up[pl.ds(first, count_up)].reshape(count_up * 128, 128)
+        return jnp.dot(spread, panels, preferred_element_type=F32)
+
+    @pl.loop(0, owners // 8 - 1)
+    def _(j):
+        arrive(8 * j, 8)
 
         @pl.loop(0, tokens_n // ROWS)
         def _(m):
             rows = pl.ds(pl.multiple_of(m * ROWS, ROWS), ROWS)
-            at, value = code[rows], shrunk[rows]
-            spread = jnp.concatenate([jnp.where(at == n, value, 0.0).astype(BF16) for n in names], axis=1)
-            panels = held_up[pl.ds(8 * j, 8)].reshape(8 * 128, 128)
-            acc[rows] += jnp.dot(spread, panels, preferred_element_type=F32)
-
-    @pl.loop(0, owners // 8)
-    def _(j):
-        apply(j)
+            acc[rows] += term(8 * j, 8, rows)
+
+    arrive(owners - 8, 8)
 
     @pl.loop(0, tokens_n // ROWS)
     def _(m):
         rows = pl.ds(pl.multiple_of(m * ROWS, ROWS), ROWS)
-        out_ref[rows] = (base_held[core, rows] + acc[rows].astype(BF16).astype(F32)).astype(BF16)
+        delta = acc[rows] + term(owners - 8, 8, rows)
+        out_ref[rows] = (base_held[core, rows] + delta.astype(BF16).astype(F32)).astype(BF16)
 
     @pl.loop(0, steps)
     def _(i):
@@ -392,12 +406,7 @@
     return pl.pallas_call(
         functools.partial(kernel, owners, groups),
         out_shape=jax.ShapeDtypeStruct((rows, units), BF16),
-        in_specs=[
-            pl.BlockSpec(memory_space=pltpu.SMEM),
-            pl.BlockSpec(memory_space=pltpu.SMEM),
-            pl.BlockSpec(memory_space=pltpu.SMEM),
-        ]
-        + [pl.BlockSpec(memory_space=pl.ANY)] * 4,
+        in_specs=[pl.BlockSpec(memory_space=pl.ANY)] * 7,
         out_specs=pl.BlockSpec(memory_space=pltpu.VMEM),
         scratch_shapes=[
             vmem(tokens.shape, BF16),
@@ -415,11 +424,14 @@
             vmem((groups, 128, 128), F32),
             vmem((groups, 128, 128), F32),
             vmem((groups, 128, 128), BF16),
+            pltpu.SMEM(request_adapter.shape, jnp.int32),
+            pltpu.SMEM(request_length.shape, jnp.int32),
+            pltpu.SMEM(adapter_panel_place.shape, jnp.int32),
             vmem((1, 128), jnp.int32),
             vmem((owners, 1, 128), jnp.int32),
             pltpu.SMEM((owners, 1, 128), jnp.int32),
             pltpu.SMEM((3, request_adapter.shape[1]), jnp.int32),
-            dma((6,)),
+            dma((9,)),
             dma((owners - 1,)),
             dma((owners - 1,)),
             dma((owners - 1,)),

time: 232 us -> 229 us (0.987)
  Pallas kernels: 229 us -> 226 us
    pallas_call x1, Pallas kernels: 229 us -> 226 us  [shards(): pl.pallas_call(functools.partial(kernel, owners, groups), out_shape=jax.S...]
where the time goes in v3:
time: 229 us; the launch traced here: 228 us
  Pallas kernels  226 us (99%)
    pallas_call x1, Pallas kernels, shards(): pl.pallas_call(functools.partial(kernel, owners, groups), out_shape=jax.S...  226 us

profile of v3, /device:TPU:33, one launch (start us, length us, event | category | flops | bytes accessed | tf_op | source)
XLA Modules:
  0.0 228.0 jit_solution(11312835766941804662)
XLA Ops:
  0.0 226.2 %routed_lora.1 = bf16[2048,128]{1,0:T(8,128)(2,1)} custom-call(s32[1,32]{1,0:T(1,128)} %adapter_hbm.1, s32[1,32]{1,0:T(1,128)} %length_hbm.1, s32[1280]{0:T(1024)} %place_hbm.1, bf16[2048,1024]{1,0:T(8,128)(2,1)} %tokens_hbm.1, bf16[1024,1024]{1,0:T(8,128)(2,1)} %weight_hbm.1, bf16[40,64,1024]{2,1,0:T(8,128)(2,1)} %down_hbm.1, bf16[40,64,128]{2,1,0:T(8,128)(2,1)} %up_hbm.1), custom_call_target="tpu_custom_call" | custom-call | tf_op jit(solution)/shard_map/routed_lora/pallas_call | solution.py:406
  226.2 1.9 copy.9

commit v4 on v3

--- a/solution.py
+++ b/solution.py
@@ -397,13 +397,17 @@
         full_copy(k).wait_send()
 
 
+def settle(values_ref, out_ref):
+    out_ref[...] = values_ref[...]
+
+
 def shards(tokens, value_weight, down_panels, up_panels, request_adapter, request_length, adapter_panel_place):
     owners, groups = lax.axis_size("wide"), lax.axis_size("grp")
     rows, features = tokens.shape
     units = up_panels.shape[2]
     dma = pltpu.SemaphoreType.DMA
     vmem = pltpu.VMEM
-    return pl.pallas_call(
+    values = pl.pallas_call(
         functools.partial(kernel, owners, groups),
         out_shape=jax.ShapeDtypeStruct((rows, units), BF16),
         in_specs=[pl.BlockSpec(memory_space=pl.ANY)] * 7,
@@ -450,6 +454,13 @@
         ),
         name="routed_lora",
     )(request_adapter, request_length, adapter_panel_place, tokens, value_weight, down_panels, up_panels)
+    return pl.pallas_call(
+        settle,
+        out_shape=jax.ShapeDtypeStruct((rows, units), BF16),
+        in_specs=[pl.BlockSpec(memory_space=pltpu.VMEM)],
+        out_specs=pl.BlockSpec(memory_space=pltpu.VMEM),
+        name="settle",
+    )(values)
 
 
 def solution(mesh):

time: 229 us -> 229 us (level)
  no operation moved by 1% of the time
where the time goes in v4:
time: 229 us; the launch traced here: 228 us
  Pallas kernels  228 us (100%)
    pallas_call x1, Pallas kernels, shards(): pl.pallas_call(functools.partial(kernel, owners, groups), out_shape=jax.S...  226 us

profile of v4, /device:TPU:33, one launch (start us, length us, event | category | flops | bytes accessed | tf_op | source)
XLA Modules:
  0.0 228.0 jit_solution(11312835766941804662)
XLA Ops:
  0.0 226.2 %routed_lora.1.values_ref = bf16[2048,128]{1,0:T(8,128)(2,1)} custom-call(s32[1,32]{1,0:T(1,128)} %adapter_hbm.1, s32[1,32]{1,0:T(1,128)} %length_hbm.1, s32[1280]{0:T(1024)} %place_hbm.1, bf16[2048,1024]{1,0:T(8,128)(2,1)} %tokens_hbm.1, bf16[1024,1024]{1,0:T(8,128)(2,1)} %weight_hbm.1, bf16[40,64,1024]{2,1,0:T(8,128)(2,1)} %down_hbm.1, ...), custom_call_target="tpu_custom_call" | custom-call | tf_op jit(solution)/shard_map/routed_lora/pallas_call | solution.py:410
  226.2 1.9 settle.1
